TPU v7x, 32 devices: a whole 2x2x4 slice. The times are simulated.
32 devices in a mesh: doc: 8 (over z, x), bkt: 4 (over y, core).
Axes of the slice: x: 2, y: 2, z: 4, core: 2. Of those that a mesh axis runs over, the one named last changes fastest.
Arguments:
- start_vectors: float32 [64, 32768], P(None, ('doc', 'bkt')), may hold values from -6 to 6
- bucket_weight: float32 [8192], P('bkt'), may hold values from 0.1 to 1
- tile_count: int32 [8, 4], P('doc', 'bkt'), may hold values from 128 to 256, as said below
- tile_coords: int32 [8, 4, 256, 2], P('doc', 'bkt'), may hold values from 0 to 31, as said below
- patterns: int32 [8, 4, 256, 128, 128], P('doc', 'bkt'), may hold values from 0 to 1
Outputs:
- eigen_block: float32 [64, 32768], P(None, ('doc', 'bkt'))
Inputs may be any that keep to these rules, and one draw needn't show every extreme that they name: `tile_count`: the largest count is exactly 256 in every draw. `tile_coords`: row tiles lie below 32, column tiles below 16; the pairs of one document band and bucket band are distinct.
All inputs are finite; a program needn't handle non-finite values.
Results may differ from a plain program's by a relative error of at most 0.018.
Values may be sent and summed in bfloat16 or wider, within the bound.
A program may use at most 128 MiB of HBM per device.

v0:
```python
import functools

import jax
import jax.numpy as jnp
from jax import lax
from jax.experimental import pallas as pl
from jax.experimental.pallas import tpu as pltpu
from jax.sharding import PartitionSpec as P

ITERS = 2


def plain_body(start_vectors, bucket_weight, tile_count, tile_coords, patterns):
    highest = lax.Precision.HIGHEST
    slot_total = patterns.shape[2]
    tile_size = patterns.shape[3]
    vector_count = start_vectors.shape[0]
    own_rows = start_vectors.shape[1]
    band_rows = own_rows * lax.axis_size("bkt")
    band_cols = bucket_weight.shape[0]
    row_tiles = band_rows // tile_size
    col_tiles = band_cols // tile_size
    total_docs = band_rows * lax.axis_size("doc")
    live_slot = (jnp.arange(slot_total) < tile_count[0, 0]).astype(jnp.int32)
    pattern_int = patterns[0, 0] * live_slot[:, None, None]
    pattern = pattern_int.astype(jnp.bfloat16)
    row_index = tile_coords[0, 0, :, 0]
    col_index = tile_coords[0, 0, :, 1]
    row_pick = jnp.arange(row_tiles)[:, None] == row_index[None, :]
    col_pick = jnp.arange(col_tiles)[:, None] == col_index[None, :]
    row_pick_f = row_pick.astype(jnp.float32)
    row_pick_b = row_pick.astype(jnp.bfloat16)
    col_pick_f = col_pick.astype(jnp.float32)
    col_pick_b = col_pick.astype(jnp.bfloat16)
    pattern_f = pattern_int.astype(jnp.float32)
    weight_tiles = bucket_weight.reshape(col_tiles, tile_size)
    slot_weight = jnp.dot(col_pick_f.T, weight_tiles, precision=highest)
    row_part = jnp.einsum("tij,tj->ti", pattern_f, slot_weight, precision=highest)
    doc_part = jnp.dot(row_pick_f, row_part, precision=highest).reshape(band_rows)
    col_part = jnp.sum(pattern_f, axis=1)
    bucket_part = jnp.dot(col_pick_f, col_part, precision=highest).reshape(band_cols)
    doc_degree = lax.psum(doc_part, "bkt")
    bucket_size = lax.psum(bucket_part.astype(jnp.bfloat16), "doc").astype(jnp.float32)
    inv_band = 1.0 / jnp.sqrt(jnp.maximum(doc_degree, 1.0))
    inv_own = lax.dynamic_slice_in_dim(inv_band, lax.axis_index("bkt") * own_rows, own_rows)
    bucket_scale = bucket_weight / jnp.maximum(bucket_size, 1.0)
    vectors = start_vectors
    for sweep_index in range(ITERS):
        scaled = (vectors * inv_own[None, :]).astype(jnp.bfloat16)
        band_vecs = lax.all_gather(scaled, "bkt", axis=1, tiled=True)
        picked = jnp.einsum(
            "rt,kri->kti",
            row_pick_b,
            band_vecs.reshape(vector_count, row_tiles, tile_size),
            preferred_element_type=jnp.float32,
        ).astype(jnp.bfloat16)
        products = jnp.einsum("kti,tij->ktj", picked, pattern, preferred_element_type=jnp.float32)
        panel_part = (
            jnp.zeros((vector_count, col_tiles, tile_size), jnp.float32)
            .at[:, col_index, :]
            .add(products)
        )
        panel_part = panel_part.reshape(vector_count, band_cols)
        panel_whole = lax.psum(panel_part, "doc")
        weighted = (panel_whole * bucket_scale[None, :]).astype(jnp.bfloat16)
        spread = jnp.einsum(
            "ct,kcj->ktj",
            col_pick_b,
            weighted.reshape(vector_count, col_tiles, tile_size),
            preferred_element_type=jnp.float32,
        ).astype(jnp.bfloat16)
        returned = jnp.einsum("ktj,tij->kti", spread, pattern, preferred_element_type=jnp.float32)
        row_terms = (
            jnp.zeros((vector_count, row_tiles, tile_size), jnp.float32)
            .at[:, row_index, :]
            .add(returned)
        )
        row_terms = row_terms.reshape(vector_count, band_rows)
        rows_own = (
            lax.psum_scatter(row_terms, "bkt", scatter_dimension=1, tiled=True) * inv_own[None, :]
        )
        gram_local = jnp.dot(rows_own, rows_own.T, precision=highest)
        gram_matrix = lax.psum(gram_local, ("doc", "bkt")) / total_docs
        factor = jnp.linalg.cholesky(gram_matrix)
        vectors = lax.linalg.triangular_solve(factor, rows_own, left_side=True, lower=True)
    return vectors


MESH = pl.DeviceIdType.MESH
F32 = jnp.float32
BF16 = jnp.bfloat16
NT = (((1,), (1,)), ((), ()))
BLOCK = 4


def kernel(
    nd,
    nb,
    slot_ref,
    start_ref,
    weight_ref,
    patterns_hbm,
    out_ref,
    tiles,
    dense,
    doc_part,
    doc_recv,
    size_part,
    size_recv,
    size_acc,
    weight_terms,
    band,
    panel_send,
    panel_recv,
    weighted,
    image_acc,
    pre_send,
    pre_recv,
    image_send,
    image_recv,
    gram_one,
    gram_one_recv,
    gram_two,
    gram_two_recv,
    inv_all,
    full,
    load_sem,
    deg_send_sem,
    deg_recv_sem,
    size_send_sem,
    size_recv_sem,
    band_send_sem,
    band_recv_sem,
    panel_send_sem,
    panel_recv_sem,
    wt_send_sem,
    wt_recv_sem,
    pre_send_sem,
    pre_recv_sem,
    image_send_sem,
    image_recv_sem,
    g1_send_sem,
    g1_recv_sem,
    g2_send_sem,
    g2_recv_sem,
    inv_send_sem,
    inv_recv_sem,
    full_send_sem,
    full_recv_sem,
):
    highest = lax.Precision.HIGHEST
    me_d = lax.axis_index("doc")
    me_b = lax.axis_index("bkt")
    tile = tiles.shape[1]
    k_vec, own_rows = start_ref.shape
    own_cols = dense.shape[2]
    row_tiles = dense.shape[1] // tile
    col_per = own_cols // tile
    col_tiles = nd * col_per
    tiles_per_own = own_rows // tile
    total_docs = own_rows * nb * nd

    def d_peer(k):
        return {"doc": lax.rem(me_d + k, nd)}

    def b_peer(k):
        return {"bkt": lax.rem(me_b + k, nb)}

    slots = tiles.shape[0] - 1
    tiles[slots] = jnp.zeros((tile, tile), jnp.int32)
    load = pltpu.make_async_copy(patterns_hbm, tiles.at[pl.ds(0, slots)], load_sem)
    load.start()
    barrier = pltpu.get_barrier_semaphore()
    for k in range(1, nb):
        pl.semaphore_signal(barrier, inc=1, device_id=b_peer(k), device_id_type=MESH)
    for k in range(1, nd):
        pl.semaphore_signal(barrier, inc=1, device_id=d_peer(k), device_id_type=MESH)
    pl.semaphore_wait(barrier, nb + nd - 2)

    def remote(src, dst, ssem, rsem, peer):
        copy = pltpu.make_async_remote_copy(
            src_ref=src, dst_ref=dst, send_sem=ssem, recv_sem=rsem,
            device_id=peer, device_id_type=MESH,
        )
        copy.start()
        return copy

    half_b, half_d = nb // 2, nd // 2
    mate_b = me_b + 1 - 2 * lax.rem(me_b, 2)
    mate_d = me_d + 1 - 2 * lax.rem(me_d, 2)
    b_mate, d_mate = {"bkt": mate_b}, {"doc": mate_d}

    def b_far(j):
        return {"bkt": lax.rem(me_b + 2 * j, nb)}

    def d_far(j):
        return {"doc": lax.rem(me_d + 2 * j, nd)}

    def source_of(me, n, j, side):
        origin = me + 1 - 2 * lax.rem(me, 2) if side else me
        return lax.rem(origin - 2 * j + n, n)

    def gather_start(buf, ssem, rsem, half, far, mate):
        sent = {}
        for j in range(1, half):
            sent[(j, 0)] = remote(buf.at[0, 0], buf.at[j, 0], ssem.at[j, 0], rsem.at[j, 0], far(j))
        sent[(0, 1)] = remote(buf.at[0, 0], buf.at[0, 1], ssem.at[0, 1], rsem.at[0, 1], mate)
        return sent

    def gather_relay(buf, ssem, rsem, j, sent, mate):
        sent[(j, 0)].wait_recv()
        sent[(j, 1)] = remote(buf.at[j, 0], buf.at[j, 1], ssem.at[j, 1], rsem.at[j, 1], mate)

    def gather_rest(sent):
        for (j, side), copy in sent.items():
            if side:
                copy.wait_recv()
        for copy in sent.values():
            copy.wait_send()

    for o in range(nd):
        left = weight_ref[o]
        terms = []
        for _ in range(3):
            terms.append(left.astype(BF16))
            left = left - terms[-1].astype(F32)
        terms = [jnp.broadcast_to(term.astype(F32), (1, own_cols)) for term in terms]
        terms.append(jnp.zeros((13, own_cols), F32))
        weight_terms[o] = jnp.concatenate(terms, axis=0).astype(BF16)
    size_acc[...] = jnp.zeros_like(size_acc)
    group = 2 if tiles_per_own % 2 == 0 else 1
    load.wait()

    @pl.loop(0, row_tiles // group)
    def _(g):
        rows = pl.ds(pl.multiple_of(g * group * tile, group * tile), group * tile)
        total = jnp.zeros((16, group * tile), F32)
        for o in range(nd):
            for h in range(col_per):
                lanes = slice(h * tile, (h + 1) * tile)
                sums = size_acc[o, :, lanes]
                blocks = []
                for u in range(group):
                    at = (g * group + u) * col_tiles + o * col_per + h
                    block = tiles[slot_ref[at]].astype(F32)
                    sums = sums + jnp.sum(block.reshape(tile // 8, 8, tile), axis=0)
                    blocks.append(block.astype(BF16))
                size_acc[o, :, lanes] = sums
                dense[o, rows, lanes] = jnp.concatenate(blocks, axis=0)
            total = total + lax.dot_general(weight_terms[o], dense[o, rows, :], NT, preferred_element_type=F32)
        summed = total[0:1] + total[1:2] + total[2:3]
        at = g * group * tile
        doc_part[at // own_rows, :, pl.ds(pl.multiple_of(lax.rem(at, own_rows), group * tile), group * tile)] = summed

    for o in range(nd):
        size_part[o] = jnp.sum(size_acc[o], axis=0, keepdims=True)

    copies = []
    for k in range(1, nb):
        q = lax.rem(me_b + k, nb)
        copies.append(remote(doc_part.at[q], doc_recv.at[k], deg_send_sem.at[k], deg_recv_sem.at[k], b_peer(k)))
    for k in range(1, nd):
        o = lax.rem(me_d + k, nd)
        copies.append(remote(size_part.at[o], size_recv.at[k], size_send_sem.at[k], size_recv_sem.at[k], d_peer(k)))
    for copy in copies:
        copy.wait()
    degree = doc_part[me_b]
    for k in range(1, nb):
        degree = degree + doc_recv[k]
    size = size_part[me_d]
    for k in range(1, nd):
        size = size + size_recv[k]
    inv_own = 1.0 / jnp.sqrt(jnp.maximum(degree, 1.0))
    scale = weight_ref[me_d] / jnp.maximum(size, 1.0)

    inv_all[me_b] = inv_own
    inv_sent = [
        remote(inv_all.at[me_b], inv_all.at[me_b], inv_send_sem.at[k], inv_recv_sem.at[k], b_peer(k))
        for k in range(1, nb)
    ]

    band[0, 0, 0] = (start_ref[...] * inv_own).astype(BF16)
    sent = gather_start(band.at[0], band_send_sem.at[0], band_recv_sem.at[0], half_b, b_far, b_mate)
    for j in range(1, half_b):
        gather_relay(band.at[0], band_send_sem.at[0], band_recv_sem.at[0], j, sent, b_mate)
    gather_rest(sent)
    for copy in inv_sent:
        copy.wait()

    for it in range(ITERS):
        def panel_of(o):
            acc = jnp.zeros((k_vec, own_cols), F32)
            for j in range(half_b):
                for side in range(2):
                    source = source_of(me_b, nb, j, side)
                    rows = pl.ds(pl.multiple_of(source * own_rows, own_rows), own_rows)
                    acc = acc + jnp.dot(band[it, j, side], dense[o, rows, :], preferred_element_type=F32)
            return acc

        @pl.loop(1, nd)
        def _(k):
            panel_send[it, k] = panel_of(lax.rem(me_d + k, nd)).astype(BF16)
            remote(panel_send.at[it, k], panel_recv.at[it, k], panel_send_sem.at[it, k], panel_recv_sem.at[it, k], d_peer(k))

        whole = panel_of(me_d)
        for k in range(1, nd):
            pltpu.make_async_remote_copy(
                src_ref=panel_send.at[it, k], dst_ref=panel_recv.at[it, k],
                send_sem=panel_send_sem.at[it, k], recv_sem=panel_recv_sem.at[it, k],
                device_id=d_peer(k), device_id_type=MESH,
            ).wait()
            whole = whole + panel_recv[it, k].astype(F32)
        weighted[it, 0, 0] = (whole * scale).astype(BF16)
        sent = gather_start(weighted.at[it], wt_send_sem.at[it], wt_recv_sem.at[it], half_d, d_far, d_mate)

        def term(q, j, side):
            rows = pl.ds(pl.multiple_of(q * own_rows, own_rows), own_rows)
            source = source_of(me_d, nd, j, side)
            return lax.dot_general(weighted[it, j, side], dense[source, rows, :], NT, preferred_element_type=F32)

        @pl.loop(0, nb)
        def _(q):
            image_acc[q] = term(q, 0, 0)

        for j in range(1, half_d):
            gather_relay(weighted.at[it], wt_send_sem.at[it], wt_recv_sem.at[it], j, sent, d_mate)
            sent[(j - 1, 1)].wait_recv()

            @pl.loop(0, nb)
            def _(q):
                image_acc[q] += term(q, j, 0) + term(q, j - 1, 1)

        last = (half_d - 1, 1)
        sent[last].wait_recv()
        for copy in sent.values():
            copy.wait_send()

        def finish(q):
            return image_acc[q] + term(q, *last)

        pre = {}
        for j in range(1, half_b):
            pre_send[it, j] = finish(lax.rem(mate_b + 2 * j, nb)).astype(BF16)
            pre[j] = remote(pre_send.at[it, j], pre_recv.at[it, j], pre_send_sem.at[it, j], pre_recv_sem.at[it, j], b_mate)
        out = []
        for j in range(1, half_b):
            both = finish(lax.rem(me_b + 2 * j, nb))
            pre[j].wait()
            image_send[it, j] = (both + pre_recv[it, j].astype(F32)).astype(BF16)
            out.append(remote(image_send.at[it, j], image_recv.at[it, j], image_send_sem.at[it, j], image_recv_sem.at[it, j], b_far(j)))
        pre_send[it, 0] = finish(mate_b).astype(BF16)
        mine = remote(pre_send.at[it, 0], pre_recv.at[it, 0], pre_send_sem.at[it, 0], pre_recv_sem.at[it, 0], b_mate)
        image = finish(me_b)
        mine.wait()
        image = image + pre_recv[it, 0].astype(F32)
        for j in range(1, half_b):
            out[j - 1].wait()
            image = image + image_recv[it, j].astype(F32)
        image = image * inv_own

        gram = lax.dot_general(image, image, NT, precision=highest, preferred_element_type=F32)
        half = k_vec // 2
        gram_one[it] = jnp.concatenate([gram[:half], gram[half:]], axis=1)
        sent = [
            remote(gram_one.at[it], gram_one_recv.at[it, k], g1_send_sem.at[it, k], g1_recv_sem.at[it, k], b_peer(k))
            for k in range(1, nb)
        ]
        folded = gram_one[it]
        for k in range(1, nb):
            sent[k - 1].wait()
            folded = folded + gram_one_recv[it, k]
        gram_two[it] = folded
        more = it + 1 < ITERS
        if more:
            full[it, 0, 0] = image
            gather = gather_start(full.at[it], full_send_sem.at[it], full_recv_sem.at[it], half_b, b_far, b_mate)
        sent = [
            remote(gram_two.at[it], gram_two_recv.at[it, k], g2_send_sem.at[it, k], g2_recv_sem.at[it, k], d_peer(k))
            for k in range(1, nd)
        ]
        for k in range(1, nd):
            sent[k - 1].wait()
            folded = folded + gram_two_recv[it, k]
        if more:
            for j in range(1, half_b):
                gather_relay(full.at[it], full_send_sem.at[it], full_recv_sem.at[it], j, gather, b_mate)
        gram = jnp.concatenate([folded[:, :k_vec], folded[:, k_vec:]], axis=0) / total_docs

        row_at = lax.broadcasted_iota(jnp.int32, (k_vec, k_vec), 0)
        col_at = lax.broadcasted_iota(jnp.int32, (k_vec, k_vec), 1)
        eye = (row_at == col_at).astype(F32)
        work = jnp.concatenate([gram, eye], axis=1)
        for at in range(0, k_vec, BLOCK):
            top = at // 8 * 8
            part = work[top:]
            below = lax.broadcasted_iota(jnp.int32, part.shape, 0)
            cols = [jnp.broadcast_to(part[:, at + m : at + m + 1], part.shape) for m in range(BLOCK)]
            for m in range(BLOCK):
                row = at - top + m
                factor = jnp.where(below > row, cols[m] * (1.0 / cols[m][row : row + 1]), 0.0)
                part = part - factor * part[row : row + 1]
                for n in range(m + 1, BLOCK):
                    cols[n] = cols[n] - factor * cols[n][row : row + 1]
            work = jnp.concatenate([work[:top], part], axis=0) if top else part
        pivots = jnp.sum(work[:, :k_vec] * eye, axis=1, keepdims=True)
        inverse = work[:, k_vec:] / jnp.sqrt(pivots)
        if more:
            for j in range(half_b):
                for side in range(2):
                    if side:
                        gather[(j, side)].wait_recv()
                    vectors = jnp.dot(inverse, full[it, j, side], precision=highest, preferred_element_type=F32)
                    band[it + 1, j, side] = (vectors * inv_all[source_of(me_b, nb, j, side)]).astype(BF16)
            for copy in gather.values():
                copy.wait_send()
        else:
            out_ref[...] = jnp.dot(inverse, image, precision=highest, preferred_element_type=F32)


def scratch_of(nd, nb, slots, tile, k_vec, own_rows, own_cols):
    dma = pltpu.SemaphoreType.DMA
    vmem = pltpu.VMEM
    fold = (k_vec // 2, 2 * k_vec)
    buffers = [
        ((slots + 1, tile, tile), jnp.int32),
        ((nd, own_rows * nb, own_cols), BF16),
        ((nb, 1, own_rows), F32),
        ((nb, 1, own_rows), F32),
        ((nd, 1, own_cols), F32),
        ((nd, 1, own_cols), F32),
        ((nd, 8, own_cols), F32),
        ((nd, 16, own_cols), BF16),
        ((ITERS, nb // 2, 2, k_vec, own_rows), BF16),
        ((ITERS, nd, k_vec, own_cols), BF16),
        ((ITERS, nd, k_vec, own_cols), BF16),
        ((ITERS, nd // 2, 2, k_vec, own_cols), BF16),
        ((nb, k_vec, own_rows), F32),
        ((ITERS, nb // 2, k_vec, own_rows), BF16),
        ((ITERS, nb // 2, k_vec, own_rows), BF16),
        ((ITERS, nb // 2, k_vec, own_rows), BF16),
        ((ITERS, nb // 2, k_vec, own_rows), BF16),
        ((ITERS,) + fold, F32),
        ((ITERS, nb) + fold, F32),
        ((ITERS,) + fold, F32),
        ((ITERS, nd) + fold, F32),
        ((nb, 1, own_rows), F32),
        ((ITERS, nb // 2, 2, k_vec, own_rows), F32),
    ]
    total = 0
    for shape, kind in buffers:
        count = jnp.dtype(kind).itemsize
        for extent in shape:
            count *= extent
        total += count
    sems = [dma]
    sems += [dma((nb,))] * 2 + [dma((nd,))] * 2
    sems += [dma((ITERS, nb // 2, 2))] * 2 + [dma((ITERS, nd))] * 2 + [dma((ITERS, nd // 2, 2))] * 2
    last = [dma((nb,))] * 2 + [dma((ITERS, nb // 2, 2))] * 2
    sems += [dma((ITERS, nb // 2))] * 4 + [dma((ITERS, nb))] * 2 + [dma((ITERS, nd))] * 2 + last
    return [vmem(shape, kind) for shape, kind in buffers] + sems, total


VMEM_BYTES = 60000 * 1024


def body(start_vectors, bucket_weight, tile_count, tile_coords, patterns):
    nd, nb = lax.axis_size("doc"), lax.axis_size("bkt")
    slots, tile = patterns.shape[2], patterns.shape[3]
    k_vec, own_rows = start_vectors.shape
    band_cols = bucket_weight.shape[0]
    own_cols = band_cols // nd
    scratch, total = scratch_of(nd, nb, slots, tile, k_vec, own_rows, own_cols)
    fits = total + 6 * k_vec * own_rows * 4 < VMEM_BYTES
    even = nd % 2 == 0 and nb % 2 == 0 and band_cols % (nd * tile) == 0 and own_rows % tile == 0 and 2 * k_vec == tile
    if not (fits and even):
        return plain_body(start_vectors, bucket_weight, tile_count, tile_coords, patterns)
    row_tiles, col_tiles = own_rows * nb // tile, band_cols // tile
    places = tile_coords[0, 0, :, 0] * col_tiles + tile_coords[0, 0, :, 1]
    slot_ids = jnp.arange(slots)
    places = jnp.where(slot_ids < tile_count[0, 0], places, -1)
    match = jnp.arange(row_tiles * col_tiles)[:, None] == places[None, :]
    found = jnp.max(jnp.where(match, slot_ids[None, :], -1), axis=1)
    slot_of = jnp.where(found >= 0, found, slots).astype(jnp.int32)
    smem = pl.BlockSpec(memory_space=pltpu.SMEM)
    vmem = pl.BlockSpec(memory_space=pltpu.VMEM)
    return pl.pallas_call(
        functools.partial(kernel, nd, nb),
        out_shape=jax.ShapeDtypeStruct((k_vec, own_rows), F32),
        in_specs=[smem, vmem, vmem, pl.BlockSpec(memory_space=pl.ANY)],
        out_specs=vmem,
        scratch_shapes=scratch,
        compiler_params=pltpu.CompilerParams(
            collective_id=0, has_side_effects=True, vmem_limit_bytes=VMEM_BYTES
        ),
        name="subspace",
    )(slot_of, start_vectors, bucket_weight.reshape(nd, 1, own_cols), patterns.reshape(slots, tile, tile))


def solution(mesh):
    in_specs = (
        P(None, ("doc", "bkt")),
        P("bkt"),
        P("doc", "bkt"),
        P("doc", "bkt", None, None),
        P("doc", "bkt", None, None, None),
    )
    out_specs = P(None, ("doc", "bkt"))
    return jax.shard_map(body, mesh=mesh, in_specs=in_specs, out_specs=out_specs, check_vma=False)
```

profile of v0, /device:TPU:0, one launch (start us, length us, event | category | flops | bytes accessed | tf_op | source)
XLA Modules:
  0.0 111.5 jit_solution(1686525282088818503)
XLA Ops:
  0.7 0.8 slice_add_fusion
  1.4 0.2 select_reduce_fusion
  1.6 0.6 compare_select_fusion.slot_ref
  2.2 107.7 %subspace.1 = f32[64,1024]{1,0:T(8,128)} custom-call(s32[512]{0:T(512)} %compare_select_fusion.slot_ref, f32[64,1024]{1,0:T(8,128)} %start_ref.1, f32[8,1,256]{2,1,0:T(1,128)} %bitcast.6, s32[256,128,128]{2,1,0:T(8,128)} %bitcast.5), custom_call_target="tpu_custom_call" | custom-call | tf_op jit(solution)/shard_map/subspace/pallas_call | solution.py:486
  109.9 1.7 %copy.8 = f32[64,1024]{1,0:T(8,128)} copy(f32[64,1024]{1,0:T(8,128)} %subspace.1) | data formatting | bytes 524288
  (1 shorter events, 0.0 us)
where the time goes:
time: 112 us
  Pallas kernels  108 us (96%)
  local copies, waits for them, and re-layouts  1.67 us (1%)
  other arithmetic  1.5 us (1%)
    pallas_call x1, Pallas kernels, body(): pl.pallas_call(functools.partial(kernel, nd, nb), out_shape=jax.ShapeDtyp...  108 us

commit v1 on v0

v1 whole, which is shorter than its diff:
```python
import functools
import types

import jax
import jax.numpy as jnp
from jax import lax
from jax.experimental import pallas as pl
from jax.experimental.pallas import tpu as pltpu
from jax.sharding import PartitionSpec as P

ITERS = 2


def plain_body(start_vectors, bucket_weight, tile_count, tile_coords, patterns):
    highest = lax.Precision.HIGHEST
    slot_total = patterns.shape[2]
    tile_size = patterns.shape[3]
    vector_count = start_vectors.shape[0]
    own_rows = start_vectors.shape[1]
    band_rows = own_rows * lax.axis_size("bkt")
    band_cols = bucket_weight.shape[0]
    row_tiles = band_rows // tile_size
    col_tiles = band_cols // tile_size
    total_docs = band_rows * lax.axis_size("doc")
    live_slot = (jnp.arange(slot_total) < tile_count[0, 0]).astype(jnp.int32)
    pattern_int = patterns[0, 0] * live_slot[:, None, None]
    pattern = pattern_int.astype(jnp.bfloat16)
    row_index = tile_coords[0, 0, :, 0]
    col_index = tile_coords[0, 0, :, 1]
    row_pick = jnp.arange(row_tiles)[:, None] == row_index[None, :]
    col_pick = jnp.arange(col_tiles)[:, None] == col_index[None, :]
    row_pick_f = row_pick.astype(jnp.float32)
    row_pick_b = row_pick.astype(jnp.bfloat16)
    col_pick_f = col_pick.astype(jnp.float32)
    col_pick_b = col_pick.astype(jnp.bfloat16)
    pattern_f = pattern_int.astype(jnp.float32)
    weight_tiles = bucket_weight.reshape(col_tiles, tile_size)
    slot_weight = jnp.dot(col_pick_f.T, weight_tiles, precision=highest)
    row_part = jnp.einsum("tij,tj->ti", pattern_f, slot_weight, precision=highest)
    doc_part = jnp.dot(row_pick_f, row_part, precision=highest).reshape(band_rows)
    col_part = jnp.sum(pattern_f, axis=1)
    bucket_part = jnp.dot(col_pick_f, col_part, precision=highest).reshape(band_cols)
    doc_degree = lax.psum(doc_part, "bkt")
    bucket_size = lax.psum(bucket_part.astype(jnp.bfloat16), "doc").astype(jnp.float32)
    inv_band = 1.0 / jnp.sqrt(jnp.maximum(doc_degree, 1.0))
    inv_own = lax.dynamic_slice_in_dim(inv_band, lax.axis_index("bkt") * own_rows, own_rows)
    bucket_scale = bucket_weight / jnp.maximum(bucket_size, 1.0)
    vectors = start_vectors
    for sweep_index in range(ITERS):
        scaled = (vectors * inv_own[None, :]).astype(jnp.bfloat16)
        band_vecs = lax.all_gather(scaled, "bkt", axis=1, tiled=True)
        picked = jnp.einsum(
            "rt,kri->kti",
            row_pick_b,
            band_vecs.reshape(vector_count, row_tiles, tile_size),
            preferred_element_type=jnp.float32,
        ).astype(jnp.bfloat16)
        products = jnp.einsum("kti,tij->ktj", picked, pattern, preferred_element_type=jnp.float32)
        panel_part = (
            jnp.zeros((vector_count, col_tiles, tile_size), jnp.float32)
            .at[:, col_index, :]
            .add(products)
        )
        panel_part = panel_part.reshape(vector_count, band_cols)
        panel_whole = lax.psum(panel_part, "doc")
        weighted = (panel_whole * bucket_scale[None, :]).astype(jnp.bfloat16)
        spread = jnp.einsum(
            "ct,kcj->ktj",
            col_pick_b,
            weighted.reshape(vector_count, col_tiles, tile_size),
            preferred_element_type=jnp.float32,
        ).astype(jnp.bfloat16)
        returned = jnp.einsum("ktj,tij->kti", spread, pattern, preferred_element_type=jnp.float32)
        row_terms = (
            jnp.zeros((vector_count, row_tiles, tile_size), jnp.float32)
            .at[:, row_index, :]
            .add(returned)
        )
        row_terms = row_terms.reshape(vector_count, band_rows)
        rows_own = (
            lax.psum_scatter(row_terms, "bkt", scatter_dimension=1, tiled=True) * inv_own[None, :]
        )
        gram_local = jnp.dot(rows_own, rows_own.T, precision=highest)
        gram_matrix = lax.psum(gram_local, ("doc", "bkt")) / total_docs
        factor = jnp.linalg.cholesky(gram_matrix)
        vectors = lax.linalg.triangular_solve(factor, rows_own, left_side=True, lower=True)
    return vectors


MESH = pl.DeviceIdType.MESH
F32 = jnp.float32
BF16 = jnp.bfloat16
I32 = jnp.int32
NT = (((1,), (1,)), ((), ()))
BLOCK = 4
CHUNKS = 8
GROUP = 16


def flip(value, k, bits):
    out = 0
    for at in range(bits):
        unit = 1 << at
        bit = lax.rem(lax.div(value, unit), 2)
        want = (k >> at) & 1 if isinstance(k, int) else lax.rem(lax.div(k, unit), 2)
        out = out + unit * (bit + want - 2 * bit * want)
    return out


def inverse_factor(gram, k_vec):
    row_at = lax.broadcasted_iota(I32, (k_vec, k_vec), 0)
    col_at = lax.broadcasted_iota(I32, (k_vec, k_vec), 1)
    eye = (row_at == col_at).astype(F32)
    work = jnp.concatenate([gram, eye], axis=1)
    for at in range(0, k_vec, BLOCK):
        top = at // 8 * 8
        part = work[top:]
        below = lax.broadcasted_iota(I32, part.shape, 0)
        cols = [jnp.broadcast_to(part[:, at + m : at + m + 1], part.shape) for m in range(BLOCK)]
        for m in range(BLOCK):
            row = at - top + m
            factor = jnp.where(below > row, cols[m] * (1.0 / cols[m][row : row + 1]), 0.0)
            part = part - factor * part[row : row + 1]
            for n in range(m + 1, BLOCK):
                cols[n] = cols[n] - factor * cols[n][row : row + 1]
        work = jnp.concatenate([work[:top], part], axis=0) if top else part
    pivots = jnp.sum(work[:, :k_vec] * eye, axis=1, keepdims=True)
    return work[:, k_vec:] / jnp.sqrt(pivots)


def kernel(names, nd, nb, count_ref, coord_ref, place_ref, start_hbm, weight_hbm, patterns_hbm, out_ref, *refs):
    s = types.SimpleNamespace(**dict(zip(names, refs, strict=True)))
    highest = lax.Precision.HIGHEST
    me_d = lax.axis_index("doc")
    me_b = lax.axis_index("bkt")
    d_bits, b_bits = nd.bit_length() - 1, nb.bit_length() - 1
    slots, tile = patterns_hbm.shape[0], patterns_hbm.shape[1]
    k_vec, own_rows = s.start.shape
    col_tiles = s.weight.shape[0]
    col_per = col_tiles // nd
    row_per = own_rows // tile
    own_cols = col_per * tile
    total_docs = own_rows * nb * nd
    nz = nd // 2

    def to(kd, kb):
        return {"doc": flip(me_d, kd, d_bits), "bkt": flip(me_b, kb, b_bits)}

    def remote(src, dst, ssem, rsem, peer):
        return pltpu.make_async_remote_copy(
            src_ref=src, dst_ref=dst, send_sem=ssem, recv_sem=rsem,
            device_id=peer, device_id_type=MESH,
        )

    def send(*args):
        copy = remote(*args)
        copy.start()
        return copy

    load_start = pltpu.make_async_copy(start_hbm, s.start, s.small_sem.at[0])
    load_start.start()
    load_weight = pltpu.make_async_copy(weight_hbm, s.weight, s.small_sem.at[1])
    load_weight.start()
    per_chunk = slots // CHUNKS

    def load(c):
        part = pl.ds(c * per_chunk, per_chunk)
        return pltpu.make_async_copy(patterns_hbm.at[part], s.tiles.at[part], s.load_sem.at[c])

    for c in range(CHUNKS):
        load(c).start()

    barrier = pltpu.get_barrier_semaphore()
    peers = [(kd, kb) for kd in range(nd) for kb in range(nb) if (kd < 2 or kb == 0) and kd + kb]
    for kd, kb in peers:
        pl.semaphore_signal(barrier, inc=1, device_id=to(kd, kb), device_id_type=MESH)

    lane = lax.broadcasted_iota(I32, (1, slots), 1)
    place = place_ref[0:1, :] * col_tiles + place_ref[1:2, :]
    place = jnp.where(lane < count_ref[0, 0], place, -1)
    across = jnp.transpose(jnp.broadcast_to(place, (tile, slots)))
    position = lax.broadcasted_iota(I32, (slots, tile), 1)
    slot_at = lax.broadcasted_iota(I32, (slots, tile), 0)
    for b in range(nb):
        found = jnp.max(jnp.where(across == position + b * tile, slot_at, -1), axis=0, keepdims=True)
        s.table[b : b + 1, :] = jnp.where(found >= 0, found, slots)
    tables = pltpu.make_async_copy(s.table, s.slot, s.small_sem.at[2])
    tables.start()
    s.bits[slots] = jnp.zeros((tile, tile), BF16)
    s.size_terms[slots] = jnp.zeros((8, tile), F32)
    s.doc_terms[slots] = jnp.zeros((8, tile), F32)

    load_weight.wait()
    for c in range(col_tiles):
        left = s.weight[c : c + 1, :]
        terms = []
        for _ in range(3):
            terms.append(left.astype(BF16).astype(F32))
            left = left - terms[-1]
        zeros = jnp.zeros((5, tile), F32)
        gap = jnp.zeros((8, tile), F32)
        eight = jnp.concatenate(terms + [zeros], axis=0)
        s.weight_terms[0, c] = jnp.concatenate([eight, gap], axis=0).astype(BF16)
        s.weight_terms[1, c] = jnp.concatenate([gap, eight], axis=0).astype(BF16)
    load_start.wait()
    s.raw[0] = s.start[...].astype(BF16)
    pl.semaphore_wait(barrier, len(peers))

    def gather_start(buf, ssem, rsem):
        return [
            send(buf.at[0], buf.at[k], ssem.at[k], rsem.at[k], to(0, k))
            for k in (2, 1)
        ]

    def gather_relay(buf, ssem, rsem, sent):
        sent[0].wait_recv()
        sent.append(send(buf.at[2], buf.at[3], ssem.at[3], rsem.at[3], to(0, 1)))

    waits = gather_start(s.raw, s.raw_send, s.raw_recv)
    raw_sent = waits


    @pl.loop(0, CHUNKS)
    def _(c):
        load(c).wait()

        @pl.loop(0, per_chunk // GROUP)
        def _(g):
            base = c * per_chunk + g * GROUP
            for u in range(0, GROUP, 2):
                pair = []
                for v in range(2):
                    at = base + u + v
                    block = s.tiles[at].astype(F32)
                    s.size_terms[at] = jnp.sum(block.reshape(tile // 8, 8, tile), axis=0)
                    pair.append(block.astype(BF16))
                    s.bits[at] = pair[v]
                left = jnp.concatenate(
                    [s.weight_terms[0, coord_ref[1, base + u]], s.weight_terms[1, coord_ref[1, base + u + 1]]], axis=1
                )
                sums = lax.dot_general(left, jnp.concatenate(pair, axis=1), NT, preferred_element_type=F32)
                s.doc_terms[base + u] = sums[:8]
                s.doc_terms[base + u + 1] = sums[8:]

    tables.wait()
    gather_relay(s.raw, s.raw_send, s.raw_recv, raw_sent)

    def slot_of(b, i, c):
        return s.slot[b, i * col_tiles + c]

    for b in range(nb):
        for i in range(row_per):
            total = s.doc_terms[slot_of(b, i, 0)]
            for c in range(1, col_tiles):
                total = total + s.doc_terms[slot_of(b, i, c)]
            s.degree_own[b * row_per + i : b * row_per + i + 1, :] = total[0:1] + total[1:2] + total[2:3]
    s.degree[me_b] = s.degree_own[...]
    degree_sent = [
        send(s.degree.at[me_b], s.degree.at[me_b], s.deg_send.at[k], s.deg_recv.at[k], to(0, k))
        for k in range(nb - 1, 0, -1)
    ]
    for c in range(col_tiles):
        total = s.size_terms[slot_of(0, 0, c)]
        for b in range(nb):
            for i in range(0 if b else 1, row_per):
                total = total + s.size_terms[slot_of(b, i, c)]
        total = jnp.sum(total, axis=0, keepdims=True)
        s.size[c // col_per, :, c % col_per * tile : (c % col_per + 1) * tile] = total
    size_sent = []
    for k in range(nd - 1, 0, -1):
        size_sent.append(
            send(s.size.at[flip(me_d, k, d_bits)], s.size_from.at[k], s.size_send.at[k], s.size_recv.at[k], to(k, 0))
        )
    for copy in degree_sent:
        copy.wait()
    degree = s.degree[0]
    for b in range(1, nb):
        degree = degree + s.degree[b]
    s.inv[...] = 1.0 / jnp.sqrt(jnp.maximum(degree, 1.0))
    for copy in raw_sent[1:]:
        copy.wait_recv()
    for k in range(nb):
        first = flip(me_b, k, b_bits) * row_per
        inv_rows = s.inv[pl.ds(pl.multiple_of(first, row_per), row_per), :]
        for i in range(row_per):
            lanes = slice(i * tile, (i + 1) * tile)
            s.band[0, k, :, lanes] = (s.raw[k, :, lanes].astype(F32) * inv_rows[i : i + 1]).astype(BF16)
    inv_own = s.inv[pl.ds(pl.multiple_of(me_b * row_per, row_per), row_per), :]

    def tiles_of(b, i, o):
        pick = [[s.bits[slot_of(b, i + u, o * col_per + h)] for h in range(col_per)] for u in range(2)]
        return jnp.concatenate([jnp.concatenate(row, axis=1) for row in pick], axis=0)

    def panel_of(it, kd, sources, acc):
        o = flip(me_d, kd, d_bits)
        for k in sources:
            b = flip(me_b, k, b_bits)
            for i in range(0, row_per, 2):
                left = s.band[it, k, :, i * tile : (i + 2) * tile]
                term = jnp.dot(left, tiles_of(b, i, o), preferred_element_type=F32)
                acc = term if acc is None else acc + term
        return acc

    def image_of(q, left, o):
        right = jnp.concatenate([tiles_of(q, i, o) for i in range(0, row_per, 2)], axis=0)
        return lax.dot_general(left, right, NT, preferred_element_type=F32)

    def gram_start(it, image):
        high = image.astype(BF16)
        low = (image - high.astype(F32)).astype(BF16)
        both = jnp.concatenate([high, low], axis=0)
        gram = lax.dot_general(both, both, NT, preferred_element_type=F32)
        gram = gram[:k_vec] + gram[k_vec:]
        gram = gram[:, :k_vec] + gram[:, k_vec:]
        half = k_vec // 2
        mine = lax.rem(me_d, 2) * nb + me_b
        s.gram_one[it, mine] = jnp.concatenate([gram[:half], gram[half:]], axis=1)
        return [
            send(s.gram_one.at[it, mine], s.gram_one.at[it, mine], s.g1_send.at[it, k], s.g1_recv.at[it, k], to(k // nb, k % nb))
            for k in range(2 * nb - 1, 0, -1)
        ]

    def gram_middle(it, sent):
        for copy in sent:
            copy.wait_recv()
        total = s.gram_one[it, 0]
        for k in range(1, 2 * nb):
            total = total + s.gram_one[it, k]
        mine = lax.div(me_d, 2)
        s.gram_two[it, mine] = total
        return [
            send(s.gram_two.at[it, mine], s.gram_two.at[it, mine], s.g2_send.at[it, k], s.g2_recv.at[it, k], to(2 * k, 0))
            for k in range(nz - 1, 0, -1)
        ]

    def gram_end(it, sent):
        for copy in sent:
            copy.wait_recv()
        total = s.gram_two[it, 0]
        for k in range(1, nz):
            total = total + s.gram_two[it, k]
        return jnp.concatenate([total[:, :k_vec], total[:, k_vec:]], axis=0) / total_docs

    waits = list(raw_sent)
    inverse = None
    for it in range(ITERS):
        first = it == 0

        def pair_copy(kz):
            return remote(
                s.pair_out.at[it, kz], s.pair_in.at[it, kz], s.pair_send.at[it, kz], s.pair_recv.at[it, kz], to(1, 0)
            )

        def line_copy(kz):
            return remote(
                s.line_out.at[it, kz], s.line_in.at[it, kz], s.line_send.at[it, kz], s.line_recv.at[it, kz], to(2 * kz, 0)
            )

        if not first:

            @pl.loop(0, nd)
            def _(kd):
                s.panel[kd] = panel_of(it, kd, (0,), None)

            band_sent[1].wait_recv()

            @pl.loop(0, nd)
            def _(kd):
                s.panel[kd] = panel_of(it, kd, (1,), s.panel[kd])

            gram_sent_two = gram_middle(it - 1, gram_sent)
            gather_relay(s.band.at[it], s.band_send, s.band_recv, band_sent)

            @pl.loop(0, nd)
            def _(kd):
                s.panel[kd] = panel_of(it, kd, (2,), s.panel[kd])

            band_sent[2].wait_recv()

        sources = tuple(range(nb)) if first else (nb - 1,)


        @pl.loop(0, nz)
        def _(at):
            kz = nz - 1 - at
            kd = 2 * kz + 1
            total = panel_of(it, kd, sources, None if first else s.panel[kd])
            s.pair_out[it, kz] = total.astype(BF16)
            pair_copy(kz).start()

        @pl.loop(0, nz - 1)
        def _(at):
            kz = nz - 1 - at
            kd = 2 * kz
            total = panel_of(it, kd, sources, None if first else s.panel[kd])
            pair_copy(kz).wait_recv()
            s.line_out[it, kz] = (total + s.pair_in[it, kz].astype(F32)).astype(BF16)
            line_copy(kz).start()

        whole = panel_of(it, 0, sources, None if first else s.panel[0])
        if not first:
            gram = gram_end(it - 1, gram_sent_two)
            inverse = inverse_factor(gram, k_vec)
            waits += gram_sent_two
        pair_copy(0).wait_recv()
        whole = whole + s.pair_in[it, 0].astype(F32)
        for kz in range(1, nz):
            line_copy(kz).wait_recv()
            whole = whole + s.line_in[it, kz].astype(F32)
        if first:
            for copy in size_sent:
                copy.wait()
            size = s.size[me_d]
            for k in range(1, nd):
                size = size + s.size_from[k]
            weight_own = jnp.concatenate([s.weight[pl.ds(me_d * col_per + h, 1), :] for h in range(col_per)], axis=1)
            scale = weight_own / jnp.maximum(size, 1.0)
        else:
            whole = jnp.dot(inverse, whole, precision=highest, preferred_element_type=F32)
        s.weighted[it, 0, 0] = (whole * scale).astype(BF16)

        def line_gather(kz):
            return remote(
                s.weighted.at[it, 0, 0], s.weighted.at[it, kz, 0], s.wt_send.at[it, kz, 0], s.wt_recv.at[it, kz, 0], to(2 * kz, 0)
            )

        def pair_gather(kz):
            return remote(
                s.weighted.at[it, kz, 0], s.weighted.at[it, kz, 1], s.wt_send.at[it, kz, 1], s.wt_recv.at[it, kz, 1], to(1, 0)
            )

        for kz in range(nz - 1, 0, -1):
            line_gather(kz).start()
        pair_gather(0).start()

        def source(kz, side):
            return flip(me_d, 2 * kz + side, d_bits)

        for q in range(nb):
            s.image[q] = image_of(q, s.weighted[it, 0, 0], me_d)

        @pl.loop(1, nz)
        def _(kz):
            line_gather(kz).wait_recv()
            pair_gather(kz).start()
            pair_gather(kz - 1).wait_recv()
            for q in range(nb):
                s.image[q] += image_of(q, s.weighted[it, kz - 1, 1], source(kz - 1, 1)) + image_of(
                    q, s.weighted[it, kz, 0], source(kz, 0)
                )

        pair_gather(nz - 1).wait_recv()

        def finish(k):
            q = flip(me_b, k, b_bits)
            return s.image[q] + image_of(q, s.weighted[it, nz - 1, 1], source(nz - 1, 1))

        def mate_copy(k):
            return remote(
                s.mate_out.at[it, k], s.mate_in.at[it, k], s.mate_send.at[it, k], s.mate_recv.at[it, k], to(0, 1)
            )

        far_copy = remote(s.far_out.at[it], s.far_in.at[it], s.far_send.at[it], s.far_recv.at[it], to(0, 2))
        s.mate_out[it, 1] = finish(3).astype(BF16)
        mate_copy(1).start()
        both = finish(2)
        mate_copy(1).wait_recv()
        s.far_out[it] = (both + s.mate_in[it, 1].astype(F32)).astype(BF16)
        far_copy.start()
        s.mate_out[it, 0] = finish(1).astype(BF16)
        mate_copy(0).start()
        image = finish(0)
        mate_copy(0).wait_recv()
        image = image + s.mate_in[it, 0].astype(F32)
        far_copy.wait_recv()
        image = image + s.far_in[it].astype(F32)
        image = jnp.concatenate(
            [image[:, i * tile : (i + 1) * tile] * inv_own[i : i + 1] for i in range(row_per)], axis=1
        )
        more = it + 1 < ITERS
        if more:
            s.band[it + 1, 0] = jnp.concatenate(
                [image[:, i * tile : (i + 1) * tile] * inv_own[i : i + 1] for i in range(row_per)], axis=1
            ).astype(BF16)
            band_sent = gather_start(s.band.at[it + 1], s.band_send, s.band_recv)
            waits += band_sent[:]
        gram_sent = gram_start(it, image)
        waits += gram_sent
        if not more:
            gram_sent_two = gram_middle(it, gram_sent)
            waits += gram_sent_two
            gram = gram_end(it, gram_sent_two)
            inverse = inverse_factor(gram, k_vec)
            out_ref[...] = jnp.dot(inverse, image, precision=highest, preferred_element_type=F32)
        for k in range(2):
            mate_copy(k).wait_send()
        far_copy.wait_send()
        for kz in range(nz):
            pair_copy(kz).wait_send()
            pair_gather(kz).wait_send()
        for kz in range(1, nz):
            line_copy(kz).wait_send()
            line_gather(kz).wait_send()
    for copy in waits:
        copy.wait_send()
    remote(s.band.at[1, 2], s.band.at[1, 3], s.band_send.at[3], s.band_recv.at[3], to(0, 1)).wait_send()


def scratch_of(nd, nb, slots, tile, k_vec, own_rows, own_cols):
    dma = pltpu.SemaphoreType.DMA
    row_tiles, col_tiles = own_rows * nb // tile, own_cols * nd // tile
    nz = nd // 2
    fold = (k_vec // 2, 2 * k_vec)
    buffers = {
        "tiles": ((slots, tile, tile), I32),
        "bits": ((slots + 1, tile, tile), BF16),
        "size_terms": ((slots + 1, 8, tile), F32),
        "doc_terms": ((slots + 1, 8, tile), F32),
        "table": ((8, tile), I32),
        "start": ((k_vec, own_rows), F32),
        "weight": ((col_tiles, tile), F32),
        "weight_terms": ((2, col_tiles, 16, tile), BF16),
        "degree_own": ((row_tiles, tile), F32),
        "degree": ((nb, row_tiles, tile), F32),
        "inv": ((row_tiles, tile), F32),
        "size": ((nd, 1, own_cols), F32),
        "size_from": ((nd, 1, own_cols), F32),
        "raw": ((nb, k_vec, own_rows), BF16),
        "band": ((ITERS, nb, k_vec, own_rows), BF16),
        "panel": ((nd, k_vec, own_cols), F32),
        "pair_out": ((ITERS, nz, k_vec, own_cols), BF16),
        "pair_in": ((ITERS, nz, k_vec, own_cols), BF16),
        "line_out": ((ITERS, nz, k_vec, own_cols), BF16),
        "line_in": ((ITERS, nz, k_vec, own_cols), BF16),
        "weighted": ((ITERS, nz, 2, k_vec, own_cols), BF16),
        "image": ((nb, k_vec, own_rows), F32),
        "mate_out": ((ITERS, 2, k_vec, own_rows), BF16),
        "mate_in": ((ITERS, 2, k_vec, own_rows), BF16),
        "far_out": ((ITERS, k_vec, own_rows), BF16),
        "far_in": ((ITERS, k_vec, own_rows), BF16),
        "gram_one": ((ITERS, 2 * nb) + fold, F32),
        "gram_two": ((ITERS, nz) + fold, F32),
    }
    total = 0
    for shape, kind in buffers.values():
        count = jnp.dtype(kind).itemsize
        for extent in shape:
            count *= extent
        total += count
    scratch = {name: pltpu.VMEM(shape, kind) for name, (shape, kind) in buffers.items()}
    scratch["slot"] = pltpu.SMEM((8, tile), I32)
    sems = {"small_sem": (3,), "load_sem": (CHUNKS,)}
    for name, shape in {
        "raw": (nb,),
        "deg": (nb,),
        "size": (nd,),
        "band": (nb,),
        "pair": (ITERS, nz),
        "line": (ITERS, nz),
        "wt": (ITERS, nz, 2),
        "mate": (ITERS, 2),
        "far": (ITERS,),
        "g1": (ITERS, 2 * nb),
        "g2": (ITERS, nz),
    }.items():
        sems[name + "_send"] = shape
        sems[name + "_recv"] = shape
    for name, shape in sems.items():
        scratch[name] = dma(shape)
    return scratch, total


VMEM_BYTES = 60000 * 1024


def body(start_vectors, bucket_weight, tile_count, tile_coords, patterns):
    nd, nb = lax.axis_size("doc"), lax.axis_size("bkt")
    slots, tile = patterns.shape[2], patterns.shape[3]
    k_vec, own_rows = start_vectors.shape
    band_cols = bucket_weight.shape[0]
    own_cols = band_cols // nd
    scratch, total = scratch_of(nd, nb, slots, tile, k_vec, own_rows, own_cols)
    fits = total + 4 * k_vec * own_rows * 4 < VMEM_BYTES
    powers = nd & (nd - 1) == 0 and nd >= 4 and nb == 4
    whole = band_cols == nd * own_cols and own_cols == 2 * tile and 2 * k_vec == tile
    table = own_rows % (2 * tile) == 0 and own_rows // tile * (band_cols // tile) == tile and own_rows // tile % 8 == 0
    if not (fits and powers and whole and table and slots % (CHUNKS * GROUP) == 0):
        return plain_body(start_vectors, bucket_weight, tile_count, tile_coords, patterns)
    smem = pl.BlockSpec(memory_space=pltpu.SMEM)
    vmem = pl.BlockSpec(memory_space=pltpu.VMEM)
    anywhere = pl.BlockSpec(memory_space=pl.ANY)
    coords = tile_coords.reshape(slots, 2).T
    return pl.pallas_call(
        functools.partial(kernel, tuple(scratch), nd, nb),
        out_shape=jax.ShapeDtypeStruct((k_vec, own_rows), F32),
        in_specs=[smem, smem, vmem, anywhere, anywhere, anywhere],
        out_specs=vmem,
        scratch_shapes=list(scratch.values()),
        compiler_params=pltpu.CompilerParams(
            collective_id=0, has_side_effects=True, vmem_limit_bytes=VMEM_BYTES
        ),
        name="subspace",
    )(tile_count, coords, coords, start_vectors, bucket_weight.reshape(band_cols // tile, tile), patterns.reshape(slots, tile, tile))


def solution(mesh):
    in_specs = (
        P(None, ("doc", "bkt")),
        P("bkt"),
        P("doc", "bkt"),
        P("doc", "bkt", None, None),
        P("doc", "bkt", None, None, None),
    )
    out_specs = P(None, ("doc", "bkt"))
    return jax.shard_map(body, mesh=mesh, in_specs=in_specs, out_specs=out_specs, check_vma=False)
```

time: 112 us -> 90.2 us (0.81)
  Pallas kernels: 108 us -> 87.7 us
  other arithmetic: 1.5 us -> 0 us
    pallas_call x1, Pallas kernels: 108 us -> 87.7 us  [body(): pl.pallas_call(functools.partial(kernel, tuple(scratch), nd, nb), out_sha...]
where the time goes in v1:
time: 90.2 us; the launch traced here: 90 us
  Pallas kernels  87.7 us (97%)
  local copies, waits for them, and re-layouts  1.67 us (2%)
    pallas_call x1, Pallas kernels, body(): pl.pallas_call(functools.partial(kernel, tuple(scratch), nd, nb), out_sha...  87.7 us

profile of v1, /device:TPU:0, one launch (start us, length us, event | category | flops | bytes accessed | tf_op | source)
XLA Modules:
  0.0 90.0 jit_solution(5496899876637323310)
XLA Ops:
  0.7 87.7 %subspace.1 = f32[64,1024]{1,0:T(8,128)} custom-call(s32[1,1]{1,0:T(1,128)S(6)} %copy.7.count_ref, s32[2,256]{1,0:T(2,128)} %bitcast.7, s32[2,256]{1,0:T(2,128)} %bitcast.8, f32[64,1024]{1,0:T(8,128)} %start_hbm.1, f32[16,128]{1,0:T(8,128)} %bitcast.6, s32[256,128,128]{2,1,0:T(8,128)} %bitcast.5), custom_call_target="tpu_custom_call" | custom-call | tf_op jit(solution)/shard_map/subspace/pallas_call | solution.py:593
  88.3 1.7 %copy.8 = f32[64,1024]{1,0:T(8,128)} copy(f32[64,1024]{1,0:T(8,128)} %subspace.1) | data formatting | bytes 524288

commit v2 on v1

--- a/solution.py
+++ b/solution.py
@@ -128,15 +128,15 @@
     return work[:, k_vec:] / jnp.sqrt(pivots)
 
 
-def kernel(names, nd, nb, count_ref, coord_ref, place_ref, start_hbm, weight_hbm, patterns_hbm, out_ref, *refs):
+def kernel(names, nd, nb, count_ref, coord_ref, place_ref, start_ref, weight_ref, patterns_hbm, out_ref, *refs):
     s = types.SimpleNamespace(**dict(zip(names, refs, strict=True)))
     highest = lax.Precision.HIGHEST
     me_d = lax.axis_index("doc")
     me_b = lax.axis_index("bkt")
     d_bits, b_bits = nd.bit_length() - 1, nb.bit_length() - 1
     slots, tile = patterns_hbm.shape[0], patterns_hbm.shape[1]
-    k_vec, own_rows = s.start.shape
-    col_tiles = s.weight.shape[0]
+    k_vec, own_rows = start_ref.shape
+    col_tiles = weight_ref.shape[0]
     col_per = col_tiles // nd
     row_per = own_rows // tile
     own_cols = col_per * tile
@@ -157,10 +157,6 @@
         copy.start()
         return copy
 
-    load_start = pltpu.make_async_copy(start_hbm, s.start, s.small_sem.at[0])
-    load_start.start()
-    load_weight = pltpu.make_async_copy(weight_hbm, s.weight, s.small_sem.at[1])
-    load_weight.start()
     per_chunk = slots // CHUNKS
 
     def load(c):
@@ -184,15 +180,15 @@
     for b in range(nb):
         found = jnp.max(jnp.where(across == position + b * tile, slot_at, -1), axis=0, keepdims=True)
         s.table[b : b + 1, :] = jnp.where(found >= 0, found, slots)
-    tables = pltpu.make_async_copy(s.table, s.slot, s.small_sem.at[2])
+    tables = pltpu.make_async_copy(s.table, s.slot, s.table_sem)
     tables.start()
     s.bits[slots] = jnp.zeros((tile, tile), BF16)
+    s.turned[slots] = jnp.zeros((tile, tile), BF16)
     s.size_terms[slots] = jnp.zeros((8, tile), F32)
     s.doc_terms[slots] = jnp.zeros((8, tile), F32)
 
-    load_weight.wait()
     for c in range(col_tiles):
-        left = s.weight[c : c + 1, :]
+        left = weight_ref[c : c + 1, :]
         terms = []
         for _ in range(3):
             terms.append(left.astype(BF16).astype(F32))
@@ -202,8 +198,7 @@
         eight = jnp.concatenate(terms + [zeros], axis=0)
         s.weight_terms[0, c] = jnp.concatenate([eight, gap], axis=0).astype(BF16)
         s.weight_terms[1, c] = jnp.concatenate([gap, eight], axis=0).astype(BF16)
-    load_start.wait()
-    s.raw[0] = s.start[...].astype(BF16)
+    s.raw[0] = start_ref[...].astype(BF16)
     pl.semaphore_wait(barrier, len(peers))
 
     def gather_start(buf, ssem, rsem):
@@ -233,12 +228,14 @@
                     at = base + u + v
                     block = s.tiles[at].astype(F32)
                     s.size_terms[at] = jnp.sum(block.reshape(tile // 8, 8, tile), axis=0)
-                    pair.append(block.astype(BF16))
-                    s.bits[at] = pair[v]
+                    block = block.astype(BF16)
+                    s.bits[at] = block
+                    pair.append(jnp.transpose(block))
+                    s.turned[at] = pair[v]
                 left = jnp.concatenate(
                     [s.weight_terms[0, coord_ref[1, base + u]], s.weight_terms[1, coord_ref[1, base + u + 1]]], axis=1
                 )
-                sums = lax.dot_general(left, jnp.concatenate(pair, axis=1), NT, preferred_element_type=F32)
+                sums = jnp.dot(left, jnp.concatenate(pair, axis=0), preferred_element_type=F32)
                 s.doc_terms[base + u] = sums[:8]
                 s.doc_terms[base + u + 1] = sums[8:]
 
@@ -302,8 +299,11 @@
         return acc
 
     def image_of(q, left, o):
-        right = jnp.concatenate([tiles_of(q, i, o) for i in range(0, row_per, 2)], axis=0)
-        return lax.dot_general(left, right, NT, preferred_element_type=F32)
+        rows = []
+        for h in range(col_per):
+            row = [s.turned[slot_of(q, i, o * col_per + h)] for i in range(row_per)]
+            rows.append(jnp.concatenate(row, axis=1))
+        return jnp.dot(left, jnp.concatenate(rows, axis=0), preferred_element_type=F32)
 
     def gram_start(it, image):
         high = image.astype(BF16)
@@ -368,13 +368,13 @@
             def _(kd):
                 s.panel[kd] = panel_of(it, kd, (1,), s.panel[kd])
 
-            gram_sent_two = gram_middle(it - 1, gram_sent)
             gather_relay(s.band.at[it], s.band_send, s.band_recv, band_sent)
 
             @pl.loop(0, nd)
             def _(kd):
                 s.panel[kd] = panel_of(it, kd, (2,), s.panel[kd])
 
+            gram_sent_two = gram_middle(it - 1, gram_sent)
             band_sent[2].wait_recv()
 
         sources = tuple(range(nb)) if first else (nb - 1,)
@@ -413,7 +413,7 @@
             size = s.size[me_d]
             for k in range(1, nd):
                 size = size + s.size_from[k]
-            weight_own = jnp.concatenate([s.weight[pl.ds(me_d * col_per + h, 1), :] for h in range(col_per)], axis=1)
+            weight_own = jnp.concatenate([weight_ref[pl.ds(me_d * col_per + h, 1), :] for h in range(col_per)], axis=1)
             scale = weight_own / jnp.maximum(size, 1.0)
         else:
             whole = jnp.dot(inverse, whole, precision=highest, preferred_element_type=F32)
@@ -514,11 +514,10 @@
     buffers = {
         "tiles": ((slots, tile, tile), I32),
         "bits": ((slots + 1, tile, tile), BF16),
+        "turned": ((slots + 1, tile, tile), BF16),
         "size_terms": ((slots + 1, 8, tile), F32),
         "doc_terms": ((slots + 1, 8, tile), F32),
         "table": ((8, tile), I32),
-        "start": ((k_vec, own_rows), F32),
-        "weight": ((col_tiles, tile), F32),
         "weight_terms": ((2, col_tiles, 16, tile), BF16),
         "degree_own": ((row_tiles, tile), F32),
         "degree": ((nb, row_tiles, tile), F32),
@@ -549,7 +548,7 @@
         total += count
     scratch = {name: pltpu.VMEM(shape, kind) for name, (shape, kind) in buffers.items()}
     scratch["slot"] = pltpu.SMEM((8, tile), I32)
-    sems = {"small_sem": (3,), "load_sem": (CHUNKS,)}
+    sems = {"load_sem": (CHUNKS,)}
     for name, shape in {
         "raw": (nb,),
         "deg": (nb,),
@@ -567,6 +566,7 @@
         sems[name + "_recv"] = shape
     for name, shape in sems.items():
         scratch[name] = dma(shape)
+    scratch["table_sem"] = dma
     return scratch, total
 
 
@@ -593,7 +593,7 @@
     return pl.pallas_call(
         functools.partial(kernel, tuple(scratch), nd, nb),
         out_shape=jax.ShapeDtypeStruct((k_vec, own_rows), F32),
-        in_specs=[smem, smem, vmem, anywhere, anywhere, anywhere],
+        in_specs=[smem, smem, vmem, vmem, vmem, anywhere],
         out_specs=vmem,
         scratch_shapes=list(scratch.values()),
         compiler_params=pltpu.CompilerParams(

time: 90.2 us -> 86.5 us (0.959)
  Pallas kernels: 87.7 us -> 84 us
    pallas_call x1, Pallas kernels: 87.7 us -> 84 us  [body(): pl.pallas_call(functools.partial(kernel, tuple(scratch), nd, nb), out_sha...]
where the time goes in v2:
time: 86.5 us; the launch traced here: 86.3 us
  Pallas kernels  84 us (97%)
  local copies, waits for them, and re-layouts  1.67 us (2%)
    pallas_call x1, Pallas kernels, body(): pl.pallas_call(functools.partial(kernel, tuple(scratch), nd, nb), out_sha...  84 us

profile of v2, /device:TPU:0, one launch (start us, length us, event | category | flops | bytes accessed | tf_op | source)
XLA Modules:
  0.0 86.3 jit_solution(7223659982832537381)
XLA Ops:
  0.7 84.0 %subspace.1 = f32[64,1024]{1,0:T(8,128)} custom-call(s32[1,1]{1,0:T(1,128)S(6)} %copy.7.count_ref, s32[2,256]{1,0:T(2,128)} %bitcast.7, s32[2,256]{1,0:T(2,128)} %bitcast.8, f32[64,1024]{1,0:T(8,128)} %start_ref.1, f32[16,128]{1,0:T(8,128)} %bitcast.6, s32[256,128,128]{2,1,0:T(8,128)} %bitcast.5), custom_call_target="tpu_custom_call" | custom-call | tf_op jit(solution)/shard_map/subspace/pallas_call | solution.py:593
  84.6 1.7 %copy.8 = f32[64,1024]{1,0:T(8,128)} copy(f32[64,1024]{1,0:T(8,128)} %subspace.1) | data formatting | bytes 524288

commit v3 on v2

--- a/solution.py
+++ b/solution.py
@@ -215,8 +215,7 @@
     raw_sent = waits
 
 
-    @pl.loop(0, CHUNKS)
-    def _(c):
+    def convert(c):
         load(c).wait()
 
         @pl.loop(0, per_chunk // GROUP)
@@ -239,8 +238,10 @@
                 s.doc_terms[base + u] = sums[:8]
                 s.doc_terms[base + u + 1] = sums[8:]
 
+    pl.loop(0, CHUNKS - 1)(convert)
+    gather_relay(s.raw, s.raw_send, s.raw_recv, raw_sent)
+    convert(CHUNKS - 1)
     tables.wait()
-    gather_relay(s.raw, s.raw_send, s.raw_recv, raw_sent)
 
     def slot_of(b, i, c):
         return s.slot[b, i * col_tiles + c]
@@ -305,7 +306,7 @@
             rows.append(jnp.concatenate(row, axis=1))
         return jnp.dot(left, jnp.concatenate(rows, axis=0), preferred_element_type=F32)
 
-    def gram_start(it, image):
+    def gram_of(image):
         high = image.astype(BF16)
         low = (image - high.astype(F32)).astype(BF16)
         both = jnp.concatenate([high, low], axis=0)
@@ -313,8 +314,21 @@
         gram = gram[:k_vec] + gram[k_vec:]
         gram = gram[:, :k_vec] + gram[:, k_vec:]
         half = k_vec // 2
+        return jnp.concatenate([gram[:half], gram[half:]], axis=1)
+
+    steps = (to(0, 1), to(0, 2), to(1, 0))
+
+    def gram_step(at, total):
+        s.gram_out[at] = total
+        return send(s.gram_out.at[at], s.gram_in.at[at], s.gs_send.at[at], s.gs_recv.at[at], steps[at])
+
+    def gram_sum(at, copy):
+        copy.wait_recv()
+        return s.gram_out[at] + s.gram_in[at]
+
+    def gram_start(it, image):
         mine = lax.rem(me_d, 2) * nb + me_b
-        s.gram_one[it, mine] = jnp.concatenate([gram[:half], gram[half:]], axis=1)
+        s.gram_one[it, mine] = gram_of(image)
         return [
             send(s.gram_one.at[it, mine], s.gram_one.at[it, mine], s.g1_send.at[it, k], s.g1_recv.at[it, k], to(k // nb, k % nb))
             for k in range(2 * nb - 1, 0, -1)
@@ -326,6 +340,9 @@
         total = s.gram_one[it, 0]
         for k in range(1, 2 * nb):
             total = total + s.gram_one[it, k]
+        return gram_line(it, total)
+
+    def gram_line(it, total):
         mine = lax.div(me_d, 2)
         s.gram_two[it, mine] = total
         return [
@@ -362,19 +379,22 @@
             def _(kd):
                 s.panel[kd] = panel_of(it, kd, (0,), None)
 
+            gram_copies = [gram_sent, gram_step(1, gram_sum(0, gram_sent))]
             band_sent[1].wait_recv()
 
             @pl.loop(0, nd)
             def _(kd):
                 s.panel[kd] = panel_of(it, kd, (1,), s.panel[kd])
 
+            gram_copies.append(gram_step(2, gram_sum(1, gram_copies[1])))
             gather_relay(s.band.at[it], s.band_send, s.band_recv, band_sent)
 
             @pl.loop(0, nd)
             def _(kd):
                 s.panel[kd] = panel_of(it, kd, (2,), s.panel[kd])
 
-            gram_sent_two = gram_middle(it - 1, gram_sent)
+            gram_sent_two = gram_line(it - 1, gram_sum(2, gram_copies[2]))
+            waits += gram_copies
             band_sent[2].wait_recv()
 
         sources = tuple(range(nb)) if first else (nb - 1,)
@@ -436,18 +456,36 @@
         def source(kz, side):
             return flip(me_d, 2 * kz + side, d_bits)
 
-        for q in range(nb):
-            s.image[q] = image_of(q, s.weighted[it, 0, 0], me_d)
-
-        @pl.loop(1, nz)
+        def line_relay():
+            return remote(
+                s.weighted.at[it, 0, 1], s.weighted.at[it, 1, 1], s.wt_send.at[it, 1, 1], s.wt_recv.at[it, 1, 1], to(2, 0)
+            )
+
+        def add_block(kz, side, fresh=False):
+            for q in range(nb):
+                term = image_of(q, s.weighted[it, kz, side], source(kz, side))
+                s.image[q] = term if fresh else s.image[q] + term
+
+        add_block(0, 0, True)
+        pair_gather(0).wait_recv()
+        line_relay().start()
+        add_block(0, 1)
+        line_gather(1).wait_recv()
+        add_block(1, 0)
+
+        @pl.loop(2, nz)
         def _(kz):
             line_gather(kz).wait_recv()
             pair_gather(kz).start()
-            pair_gather(kz - 1).wait_recv()
-            for q in range(nb):
-                s.image[q] += image_of(q, s.weighted[it, kz - 1, 1], source(kz - 1, 1)) + image_of(
-                    q, s.weighted[it, kz, 0], source(kz, 0)
-                )
+            add_block(kz, 0)
+
+        line_relay().wait_recv()
+        add_block(1, 1)
+
+        @pl.loop(2, nz - 1)
+        def _(kz):
+            pair_gather(kz).wait_recv()
+            add_block(kz, 1)
 
         pair_gather(nz - 1).wait_recv()
 
@@ -484,9 +522,10 @@
             ).astype(BF16)
             band_sent = gather_start(s.band.at[it + 1], s.band_send, s.band_recv)
             waits += band_sent[:]
-        gram_sent = gram_start(it, image)
-        waits += gram_sent
-        if not more:
+            gram_sent = gram_step(0, gram_of(image))
+        else:
+            gram_sent = gram_start(it, image)
+            waits += gram_sent
             gram_sent_two = gram_middle(it, gram_sent)
             waits += gram_sent_two
             gram = gram_end(it, gram_sent_two)
@@ -497,7 +536,7 @@
         far_copy.wait_send()
         for kz in range(nz):
             pair_copy(kz).wait_send()
-            pair_gather(kz).wait_send()
+            (line_relay() if kz == 1 else pair_gather(kz)).wait_send()
         for kz in range(1, nz):
             line_copy(kz).wait_send()
             line_gather(kz).wait_send()
@@ -537,6 +576,8 @@
         "mate_in": ((ITERS, 2, k_vec, own_rows), BF16),
         "far_out": ((ITERS, k_vec, own_rows), BF16),
         "far_in": ((ITERS, k_vec, own_rows), BF16),
+        "gram_out": ((3,) + fold, F32),
+        "gram_in": ((3,) + fold, F32),
         "gram_one": ((ITERS, 2 * nb) + fold, F32),
         "gram_two": ((ITERS, nz) + fold, F32),
     }
@@ -559,6 +600,7 @@
         "wt": (ITERS, nz, 2),
         "mate": (ITERS, 2),
         "far": (ITERS,),
+        "gs": (3,),
         "g1": (ITERS, 2 * nb),
         "g2": (ITERS, nz),
     }.items():

time: 86.5 us -> 81.7 us (0.945)
  Pallas kernels: 84 us -> 79.3 us
    pallas_call x1, Pallas kernels: 84 us -> 79.3 us  [body(): pl.pallas_call(functools.partial(kernel, tuple(scratch), nd, nb), out_sha...]
where the time goes in v3:
time: 81.7 us; the launch traced here: 81.6 us
  Pallas kernels  79.3 us (97%)
  local copies, waits for them, and re-layouts  1.67 us (2%)
    pallas_call x1, Pallas kernels, body(): pl.pallas_call(functools.partial(kernel, tuple(scratch), nd, nb), out_sha...  79.3 us
    unnamed x1, local copies, waits for them, and re-layouts  1.67 us

profile of v3, /device:TPU:0, one launch (start us, length us, event | category | flops | bytes accessed | tf_op | source)
XLA Modules:
  0.0 81.6 jit_solution(2623204793813814028)
XLA Ops:
  0.7 79.3 %subspace.1 = f32[64,1024]{1,0:T(8,128)} custom-call(s32[1,1]{1,0:T(1,128)S(6)} %copy.7.count_ref, s32[2,256]{1,0:T(2,128)} %bitcast.7, s32[2,256]{1,0:T(2,128)} %bitcast.8, f32[64,1024]{1,0:T(8,128)} %start_ref.1, f32[16,128]{1,0:T(8,128)} %bitcast.6, s32[256,128,128]{2,1,0:T(8,128)} %bitcast.5), custom_call_target="tpu_custom_call" | custom-call | tf_op jit(solution)/shard_map/subspace/pallas_call | solution.py:635
  79.9 1.7 %copy.8 = f32[64,1024]{1,0:T(8,128)} copy(f32[64,1024]{1,0:T(8,128)} %subspace.1) | data formatting | bytes 524288

commit v4 on v3

--- a/solution.py
+++ b/solution.py
@@ -92,7 +92,7 @@
 BF16 = jnp.bfloat16
 I32 = jnp.int32
 NT = (((1,), (1,)), ((), ()))
-BLOCK = 4
+BLOCK = 8
 CHUNKS = 8
 GROUP = 16
 
@@ -128,7 +128,7 @@
     return work[:, k_vec:] / jnp.sqrt(pivots)
 
 
-def kernel(names, nd, nb, count_ref, coord_ref, place_ref, start_ref, weight_ref, patterns_hbm, out_ref, *refs):
+def kernel(names, nd, nb, count_ref, coord_ref, place_ref, start_ref, weight_ref, patterns_hbm, out_ref, image_hbm, *refs):
     s = types.SimpleNamespace(**dict(zip(names, refs, strict=True)))
     highest = lax.Precision.HIGHEST
     me_d = lax.axis_index("doc")
@@ -140,6 +140,8 @@
     col_per = col_tiles // nd
     row_per = own_rows // tile
     own_cols = col_per * tile
+    half_per = row_per // 2
+    half_rows = half_per * tile
     total_docs = own_rows * nb * nd
     nz = nd // 2
 
@@ -282,7 +284,8 @@
         inv_rows = s.inv[pl.ds(pl.multiple_of(first, row_per), row_per), :]
         for i in range(row_per):
             lanes = slice(i * tile, (i + 1) * tile)
-            s.band[0, k, :, lanes] = (s.raw[k, :, lanes].astype(F32) * inv_rows[i : i + 1]).astype(BF16)
+            half_lanes = slice(i % half_per * tile, (i % half_per + 1) * tile)
+            s.band[0, k, i // half_per, :, half_lanes] = (s.raw[k, :, lanes].astype(F32) * inv_rows[i : i + 1]).astype(BF16)
     inv_own = s.inv[pl.ds(pl.multiple_of(me_b * row_per, row_per), row_per), :]
 
     def tiles_of(b, i, o):
@@ -294,15 +297,15 @@
         for k in sources:
             b = flip(me_b, k, b_bits)
             for i in range(0, row_per, 2):
-                left = s.band[it, k, :, i * tile : (i + 2) * tile]
+                left = s.band[it, k, i // half_per, :, i % half_per * tile : (i % half_per + 2) * tile]
                 term = jnp.dot(left, tiles_of(b, i, o), preferred_element_type=F32)
                 acc = term if acc is None else acc + term
         return acc
 
-    def image_of(q, left, o):
+    def image_of(q, left, o, first=0, last=row_per):
         rows = []
         for h in range(col_per):
-            row = [s.turned[slot_of(q, i, o * col_per + h)] for i in range(row_per)]
+            row = [s.turned[slot_of(q, i, o * col_per + h)] for i in range(first, last)]
             rows.append(jnp.concatenate(row, axis=1))
         return jnp.dot(left, jnp.concatenate(rows, axis=0), preferred_element_type=F32)
 
@@ -316,7 +319,7 @@
         half = k_vec // 2
         return jnp.concatenate([gram[:half], gram[half:]], axis=1)
 
-    steps = (to(0, 1), to(0, 2), to(1, 0))
+    steps = (to(0, 1), to(1, 0), to(0, 2))
 
     def gram_step(at, total):
         s.gram_out[at] = total
@@ -358,6 +361,13 @@
             total = total + s.gram_two[it, k]
         return jnp.concatenate([total[:, :k_vec], total[:, k_vec:]], axis=0) / total_docs
 
+    def band_copy(k, h):
+        if k == 3:
+            src, peer = s.band.at[1, 2, h], to(0, 1)
+        else:
+            src, peer = s.band.at[1, 0, h], to(0, k)
+        return remote(src, s.band.at[1, k, h], s.band_send.at[k, h], s.band_recv.at[k, h], peer)
+
     waits = list(raw_sent)
     inverse = None
     for it in range(ITERS):
@@ -375,27 +385,27 @@
 
         if not first:
 
-            @pl.loop(0, nd)
-            def _(kd):
+            for kd in range(nd):
                 s.panel[kd] = panel_of(it, kd, (0,), None)
 
             gram_copies = [gram_sent, gram_step(1, gram_sum(0, gram_sent))]
-            band_sent[1].wait_recv()
-
-            @pl.loop(0, nd)
-            def _(kd):
+            for h in range(2):
+                band_copy(1, h).wait_recv()
+
+            for kd in range(nd):
                 s.panel[kd] = panel_of(it, kd, (1,), s.panel[kd])
 
+            band_copy(2, 0).wait_recv()
+            band_copy(3, 0).start()
             gram_copies.append(gram_step(2, gram_sum(1, gram_copies[1])))
-            gather_relay(s.band.at[it], s.band_send, s.band_recv, band_sent)
-
-            @pl.loop(0, nd)
-            def _(kd):
+            band_copy(2, 1).wait_recv()
+            band_copy(3, 1).start()
+
+            for kd in range(nd):
                 s.panel[kd] = panel_of(it, kd, (2,), s.panel[kd])
 
-            gram_sent_two = gram_line(it - 1, gram_sum(2, gram_copies[2]))
-            waits += gram_copies
-            band_sent[2].wait_recv()
+            for h in range(2):
+                band_copy(3, h).wait_recv()
 
         sources = tuple(range(nb)) if first else (nb - 1,)
 
@@ -407,6 +417,10 @@
             total = panel_of(it, kd, sources, None if first else s.panel[kd])
             s.pair_out[it, kz] = total.astype(BF16)
             pair_copy(kz).start()
+
+        if not first:
+            gram_sent_two = gram_line(it - 1, gram_sum(2, gram_copies[2]))
+            waits += gram_copies
 
         @pl.loop(0, nz - 1)
         def _(at):
@@ -489,51 +503,66 @@
 
         pair_gather(nz - 1).wait_recv()
 
-        def finish(k):
+        def finish(k, h):
             q = flip(me_b, k, b_bits)
-            return s.image[q] + image_of(q, s.weighted[it, nz - 1, 1], source(nz - 1, 1))
-
-        def mate_copy(k):
+            term = image_of(q, s.weighted[it, nz - 1, 1], source(nz - 1, 1), h * half_per, (h + 1) * half_per)
+            return s.image[q, :, h * half_rows : (h + 1) * half_rows] + term
+
+        def mate_copy(k, h):
             return remote(
-                s.mate_out.at[it, k], s.mate_in.at[it, k], s.mate_send.at[it, k], s.mate_recv.at[it, k], to(0, 1)
+                s.mate_out.at[it, k, h], s.mate_in.at[it, k, h], s.mate_send.at[it, k, h], s.mate_recv.at[it, k, h], to(0, 1)
             )
 
-        far_copy = remote(s.far_out.at[it], s.far_in.at[it], s.far_send.at[it], s.far_recv.at[it], to(0, 2))
-        s.mate_out[it, 1] = finish(3).astype(BF16)
-        mate_copy(1).start()
-        both = finish(2)
-        mate_copy(1).wait_recv()
-        s.far_out[it] = (both + s.mate_in[it, 1].astype(F32)).astype(BF16)
-        far_copy.start()
-        s.mate_out[it, 0] = finish(1).astype(BF16)
-        mate_copy(0).start()
-        image = finish(0)
-        mate_copy(0).wait_recv()
-        image = image + s.mate_in[it, 0].astype(F32)
-        far_copy.wait_recv()
-        image = image + s.far_in[it].astype(F32)
-        image = jnp.concatenate(
-            [image[:, i * tile : (i + 1) * tile] * inv_own[i : i + 1] for i in range(row_per)], axis=1
-        )
+        def far_copy(h):
+            return remote(s.far_out.at[it, h], s.far_in.at[it, h], s.far_send.at[it, h], s.far_recv.at[it, h], to(0, 2))
+
+        def weigh(value, h):
+            parts = [
+                value[:, i * tile : (i + 1) * tile] * inv_own[h * half_per + i : h * half_per + i + 1]
+                for i in range(half_per)
+            ]
+            return jnp.concatenate(parts, axis=1)
+
+        for h in range(2):
+            s.mate_out[it, 1, h] = finish(3, h).astype(BF16)
+            mate_copy(1, h).start()
+        for h in range(2):
+            both = finish(2, h)
+            mate_copy(1, h).wait_recv()
+            s.far_out[it, h] = (both + s.mate_in[it, 1, h].astype(F32)).astype(BF16)
+            far_copy(h).start()
+        for h in range(2):
+            s.mate_out[it, 0, h] = finish(1, h).astype(BF16)
+            mate_copy(0, h).start()
+        halves = [finish(0, h) for h in range(2)]
         more = it + 1 < ITERS
+        for h in range(2):
+            mate_copy(0, h).wait_recv()
+            far_copy(h).wait_recv()
+            halves[h] = weigh(halves[h] + s.mate_in[it, 0, h].astype(F32) + s.far_in[it, h].astype(F32), h)
+            if more:
+                s.band[it + 1, 0, h] = weigh(halves[h], h).astype(BF16)
+                for k in (2, 1):
+                    band_copy(k, h).start()
+        image = jnp.concatenate(halves, axis=1)
         if more:
-            s.band[it + 1, 0] = jnp.concatenate(
-                [image[:, i * tile : (i + 1) * tile] * inv_own[i : i + 1] for i in range(row_per)], axis=1
-            ).astype(BF16)
-            band_sent = gather_start(s.band.at[it + 1], s.band_send, s.band_recv)
-            waits += band_sent[:]
             gram_sent = gram_step(0, gram_of(image))
         else:
+            s.final[...] = image
+            store = pltpu.make_async_copy(s.final, image_hbm, s.store_sem)
+            store.start()
             gram_sent = gram_start(it, image)
             waits += gram_sent
             gram_sent_two = gram_middle(it, gram_sent)
             waits += gram_sent_two
             gram = gram_end(it, gram_sent_two)
             inverse = inverse_factor(gram, k_vec)
-            out_ref[...] = jnp.dot(inverse, image, precision=highest, preferred_element_type=F32)
-        for k in range(2):
-            mate_copy(k).wait_send()
-        far_copy.wait_send()
+            out_ref[...] = inverse
+            store.wait()
+        for h in range(2):
+            for k in range(2):
+                mate_copy(k, h).wait_send()
+            far_copy(h).wait_send()
         for kz in range(nz):
             pair_copy(kz).wait_send()
             (line_relay() if kz == 1 else pair_gather(kz)).wait_send()
@@ -542,7 +571,9 @@
             line_gather(kz).wait_send()
     for copy in waits:
         copy.wait_send()
-    remote(s.band.at[1, 2], s.band.at[1, 3], s.band_send.at[3], s.band_recv.at[3], to(0, 1)).wait_send()
+    for k in range(1, nb):
+        for h in range(2):
+            band_copy(k, h).wait_send()
 
 
 def scratch_of(nd, nb, slots, tile, k_vec, own_rows, own_cols):
@@ -564,7 +595,7 @@
         "size": ((nd, 1, own_cols), F32),
         "size_from": ((nd, 1, own_cols), F32),
         "raw": ((nb, k_vec, own_rows), BF16),
-        "band": ((ITERS, nb, k_vec, own_rows), BF16),
+        "band": ((ITERS, nb, 2, k_vec, own_rows // 2), BF16),
         "panel": ((nd, k_vec, own_cols), F32),
         "pair_out": ((ITERS, nz, k_vec, own_cols), BF16),
         "pair_in": ((ITERS, nz, k_vec, own_cols), BF16),
@@ -572,10 +603,11 @@
         "line_in": ((ITERS, nz, k_vec, own_cols), BF16),
         "weighted": ((ITERS, nz, 2, k_vec, own_cols), BF16),
         "image": ((nb, k_vec, own_rows), F32),
-        "mate_out": ((ITERS, 2, k_vec, own_rows), BF16),
-        "mate_in": ((ITERS, 2, k_vec, own_rows), BF16),
-        "far_out": ((ITERS, k_vec, own_rows), BF16),
-        "far_in": ((ITERS, k_vec, own_rows), BF16),
+        "mate_out": ((ITERS, 2, 2, k_vec, own_rows // 2), BF16),
+        "mate_in": ((ITERS, 2, 2, k_vec, own_rows // 2), BF16),
+        "far_out": ((ITERS, 2, k_vec, own_rows // 2), BF16),
+        "far_in": ((ITERS, 2, k_vec, own_rows // 2), BF16),
+        "final": ((k_vec, own_rows), F32),
         "gram_out": ((3,) + fold, F32),
         "gram_in": ((3,) + fold, F32),
         "gram_one": ((ITERS, 2 * nb) + fold, F32),
@@ -594,12 +626,12 @@
         "raw": (nb,),
         "deg": (nb,),
         "size": (nd,),
-        "band": (nb,),
+        "band": (nb, 2),
         "pair": (ITERS, nz),
         "line": (ITERS, nz),
         "wt": (ITERS, nz, 2),
-        "mate": (ITERS, 2),
-        "far": (ITERS,),
+        "mate": (ITERS, 2, 2),
+        "far": (ITERS, 2),
         "gs": (3,),
         "g1": (ITERS, 2 * nb),
         "g2": (ITERS, nz),
@@ -609,6 +641,7 @@
     for name, shape in sems.items():
         scratch[name] = dma(shape)
     scratch["table_sem"] = dma
+    scratch["store_sem"] = dma
     return scratch, total
 
 
@@ -632,17 +665,18 @@
     vmem = pl.BlockSpec(memory_space=pltpu.VMEM)
     anywhere = pl.BlockSpec(memory_space=pl.ANY)
     coords = tile_coords.reshape(slots, 2).T
-    return pl.pallas_call(
+    inverse, image = pl.pallas_call(
         functools.partial(kernel, tuple(scratch), nd, nb),
-        out_shape=jax.ShapeDtypeStruct((k_vec, own_rows), F32),
+        out_shape=[jax.ShapeDtypeStruct((k_vec, k_vec), F32), jax.ShapeDtypeStruct((k_vec, own_rows), F32)],
         in_specs=[smem, smem, vmem, vmem, vmem, anywhere],
-        out_specs=vmem,
+        out_specs=[vmem, anywhere],
         scratch_shapes=list(scratch.values()),
         compiler_params=pltpu.CompilerParams(
             collective_id=0, has_side_effects=True, vmem_limit_bytes=VMEM_BYTES
         ),
         name="subspace",
     )(tile_count, coords, coords, start_vectors, bucket_weight.reshape(band_cols // tile, tile), patterns.reshape(slots, tile, tile))
+    return jnp.dot(inverse, image, precision=lax.Precision.HIGH)
 
 
 def solution(mesh):

time: 81.7 us -> 79 us (0.967)
  Pallas kernels: 79.3 us -> 76.3 us
  matrix products: 0 us -> 1.92 us
  local copies, waits for them, and re-layouts: 1.67 us -> 0 us
    pallas_call x1, Pallas kernels: 79.3 us -> 76.3 us  [body(): pl.pallas_call(functools.partial(kernel, tuple(scratch), nd, nb), out_sha...]
    dot_general x0 -> x1, matrix products: none -> 1.92 us  [body(): return jnp.dot(inverse, image, precision=lax.Precision.HIGH)]
    unnamed x1 -> x0, local copies, waits for them, and re-layouts: 1.67 us -> none
where the time goes in v4:
time: 79 us; the launch traced here: 78.8 us
  Pallas kernels  76.3 us (97%)
  matrix products  1.92 us (2%)
    pallas_call x1, Pallas kernels, body(): pl.pallas_call(functools.partial(kernel, tuple(scratch), nd, nb), out_sha...  76.3 us
    dot_general x1, matrix products, body(): return jnp.dot(inverse, image, precision=lax.Precision.HIGH)  1.92 us

profile of v4, /device:TPU:0, one launch (start us, length us, event | category | flops | bytes accessed | tf_op | source)
XLA Modules:
  0.0 78.8 jit_solution(13918751812104723135)
XLA Ops:
  0.7 76.3 %subspace.1 = (f32[64,64]{1,0:T(8,128)}, f32[64,1024]{1,0:T(8,128)}) custom-call(s32[1,1]{1,0:T(1,128)S(6)} %copy.6.count_ref, s32[2,256]{1,0:T(2,128)} %bitcast.9, s32[2,256]{1,0:T(2,128)} %bitcast.10, f32[64,1024]{1,0:T(8,128)} %start_ref.1, f32[16,128]{1,0:T(8,128)} %bitcast.8, s32[256,128,128]{2,1,0:T(8,128)} %bitcast.7), custom_call_target="tpu_custom_call" | custom-call | tf_op jit(solution)/shard_map/subspace/pallas_call | solution.py:668
  76.9 1.9 %fusion = f32[64,1024]{1,0:T(8,128)} fusion(f32[64,64]{1,0:T(8,128)} %get-tuple-element.7, f32[64,1024]{1,0:T(8,128)} %get-tuple-element.8), kind=kOutput, calls=%fused_computation | convolution fusion | flops 25165824 | bytes 540672 | tf_op jit(solution)/shard_map/dot_general | solution.py:679

commit v5 on v4

--- a/solution.py
+++ b/solution.py
@@ -92,7 +92,7 @@
 BF16 = jnp.bfloat16
 I32 = jnp.int32
 NT = (((1,), (1,)), ((), ()))
-BLOCK = 8
+BLOCK = 16
 CHUNKS = 8
 GROUP = 16
 
@@ -309,11 +309,13 @@
             rows.append(jnp.concatenate(row, axis=1))
         return jnp.dot(left, jnp.concatenate(rows, axis=0), preferred_element_type=F32)
 
-    def gram_of(image):
+    def gram_part(image):
         high = image.astype(BF16)
         low = (image - high.astype(F32)).astype(BF16)
         both = jnp.concatenate([high, low], axis=0)
-        gram = lax.dot_general(both, both, NT, preferred_element_type=F32)
+        return lax.dot_general(both, both, NT, preferred_element_type=F32)
+
+    def gram_of(gram):
         gram = gram[:k_vec] + gram[k_vec:]
         gram = gram[:, :k_vec] + gram[:, k_vec:]
         half = k_vec // 2
@@ -329,9 +331,9 @@
         copy.wait_recv()
         return s.gram_out[at] + s.gram_in[at]
 
-    def gram_start(it, image):
+    def gram_start(it, gram):
         mine = lax.rem(me_d, 2) * nb + me_b
-        s.gram_one[it, mine] = gram_of(image)
+        s.gram_one[it, mine] = gram_of(gram)
         return [
             send(s.gram_one.at[it, mine], s.gram_one.at[it, mine], s.g1_send.at[it, k], s.g1_recv.at[it, k], to(k // nb, k % nb))
             for k in range(2 * nb - 1, 0, -1)
@@ -544,14 +546,15 @@
                 s.band[it + 1, 0, h] = weigh(halves[h], h).astype(BF16)
                 for k in (2, 1):
                     band_copy(k, h).start()
+            gram = gram_part(halves[h]) if h == 0 else gram + gram_part(halves[h])
         image = jnp.concatenate(halves, axis=1)
         if more:
-            gram_sent = gram_step(0, gram_of(image))
+            gram_sent = gram_step(0, gram_of(gram))
         else:
             s.final[...] = image
             store = pltpu.make_async_copy(s.final, image_hbm, s.store_sem)
             store.start()
-            gram_sent = gram_start(it, image)
+            gram_sent = gram_start(it, gram)
             waits += gram_sent
             gram_sent_two = gram_middle(it, gram_sent)
             waits += gram_sent_two

time: 79 us -> 78.8 us (level)
  no operation moved by 1% of the time
where the time goes in v5:
time: 78.8 us; the launch traced here: 78.6 us
  Pallas kernels  76 us (96%)
  matrix products  1.92 us (2%)
    pallas_call x1, Pallas kernels, body(): pl.pallas_call(functools.partial(kernel, tuple(scratch), nd, nb), out_sha...  76 us
    dot_general x1, matrix products, body(): return jnp.dot(inverse, image, precision=lax.Precision.HIGH)  1.92 us

profile of v5, /device:TPU:0, one launch (start us, length us, event | category | flops | bytes accessed | tf_op | source)
XLA Modules:
  0.0 78.6 jit_solution(3649088829155818157)
XLA Ops:
  0.7 76.0 %subspace.1 = (f32[64,64]{1,0:T(8,128)}, f32[64,1024]{1,0:T(8,128)}) custom-call(s32[1,1]{1,0:T(1,128)S(6)} %copy.6.count_ref, s32[2,256]{1,0:T(2,128)} %bitcast.9, s32[2,256]{1,0:T(2,128)} %bitcast.10, f32[64,1024]{1,0:T(8,128)} %start_ref.1, f32[16,128]{1,0:T(8,128)} %bitcast.8, s32[256,128,128]{2,1,0:T(8,128)} %bitcast.7), custom_call_target="tpu_custom_call" | custom-call | tf_op jit(solution)/shard_map/subspace/pallas_call | solution.py:671
  76.7 1.9 %fusion = f32[64,1024]{1,0:T(8,128)} fusion(f32[64,64]{1,0:T(8,128)} %get-tuple-element.7, f32[64,1024]{1,0:T(8,128)} %get-tuple-element.8), kind=kOutput, calls=%fused_computation | convolution fusion | flops 25165824 | bytes 540672 | tf_op jit(solution)/shard_map/dot_general | solution.py:682
